TPU v7x, 256 devices: a whole 4x4x8 slice. The times are simulated.
256 devices in a mesh: lx: 8 (over z), ly: 8 (over x, y_lo), blk: 4 (over y_hi, core).
Axes of the slice: x: 4, y: 4 (y_hi: 2, y_lo: 2; y = y_hi * 2 + y_lo), z: 8, core: 2. Of those that a mesh axis runs over, the one named last changes fastest.
Arguments:
- block_vectors: float32 [32, 1024, 2048], P('blk', 'lx', 'ly'), may hold values from -6 to 6
- search_vectors: float32 [256, 1024, 2048], P('blk', 'lx', 'ly'), may hold values from -6 to 6
- onsite_energy: float32 [1024, 2048], P('lx', 'ly'), may hold values from -1 to 1
- site_mask: int32 [1024, 2048], P('lx', 'ly'), may hold values 0 or 1
- filter_coefs: float32 [5], replicated, may hold values from -1 to 1
Outputs:
- projected: float32 [2, 32, 256], P(None, None, 'blk')
Inputs may be any that keep to these rules, and one draw needn't show every extreme that they name: `site_mask`: 1 marks a present site, 0 a vacancy.
All inputs are finite; a program needn't handle non-finite values. No bound on the sum of `site_mask` on one device may be relied on, other than what follows from the above.
Results may differ from a plain program's by a relative error of at most 0.00016.
Values sent between devices are 32-bit elements; how exact they have to be, the bound alone decides.
No kernel may reach another device: no remote copies, remote signals or barrier semaphores. Data moves between devices by JAX's collectives and lax.ppermute only.
A program may use at most 64 MiB of HBM per device.

v0:
```python
import math
import jax
import jax.numpy as jnp
from jax import lax
from jax.sharding import PartitionSpec as P


def extended(block, sides, width):
    for axis, dim in sides:
        count = lax.axis_size(axis)
        forward = [(i, i + 1) for i in range(count - 1)]
        backward = [(target, source) for source, target in forward]
        low = lax.ppermute(
            lax.slice_in_dim(block, block.shape[dim] - width, None, axis=dim), axis, forward
        )
        high = lax.ppermute(lax.slice_in_dim(block, 0, width, axis=dim), axis, backward)
        block = jnp.concatenate([low, block, high], axis=dim)
    return block


def scaled_step(padded, onsite, present):
    nrows, ncols = onsite.shape
    row_index = lax.broadcasted_iota(jnp.int32, (nrows, ncols), 0)
    col_index = lax.broadcasted_iota(jnp.int32, (nrows, ncols), 1)
    even_sites = (row_index + col_index) % 2 == 0
    centre = padded[..., 1:-1, 1:-1]
    left_side = padded[..., 1:-1, :-2]
    right_side = padded[..., 1:-1, 2:]
    upper_side = padded[..., :-2, 1:-1]
    lower_side = padded[..., 2:, 1:-1]
    vertical = jnp.where(even_sites, lower_side, upper_side)
    return present * (onsite * centre - (left_side + right_side + vertical)) * 0.25


def gram_rows(stacked, search_vectors):
    stacks, members, nrows, ncols = stacked.shape
    flat = stacked.reshape(stacks * members, nrows * ncols)
    search_flat = search_vectors.reshape(search_vectors.shape[0], nrows * ncols)
    result = lax.dot_general(
        flat,
        search_flat,
        (((1,), (1,)), ((), ())),
        precision=lax.Precision.HIGHEST,
        preferred_element_type=jnp.float32,
    )
    return result.reshape(stacks, members, search_vectors.shape[0])


def shards(block_vectors, search_vectors, onsite_energy, site_mask, filter_coefs):
    present = site_mask.astype(jnp.float32)
    current = block_vectors * present
    filtered = filter_coefs[0] * current
    degree = filter_coefs.shape[0] - 1
    before = current
    for order in range(1, degree + 1):
        padded_field = extended(current, (("lx", 1), ("ly", 2)), 1)
        image = scaled_step(padded_field, onsite_energy, present)
        following = image if order == 1 else 2.0 * image - before
        before, current = (current, following)
        filtered = filtered + filter_coefs[order] * current
    nrows, ncols = onsite_energy.shape
    scale_factor = 1.0 / math.sqrt(nrows * ncols * lax.axis_size("lx") * lax.axis_size("ly"))
    padded_field = extended(filtered, (("lx", 1), ("ly", 2)), 1)
    image = scaled_step(padded_field, onsite_energy, present)
    paired = jnp.stack([filtered, image])
    partial_gram = gram_rows(lax.all_gather(paired, "blk", axis=1, tiled=True), search_vectors)
    total = lax.psum(partial_gram, ("lx", "ly"))
    return total * scale_factor


def solution(mesh):
    placed = (P("blk", "lx", "ly"), P("blk", "lx", "ly"), P("lx", "ly"), P("lx", "ly"), P())
    return jax.shard_map(
        shards, mesh=mesh, in_specs=placed, out_specs=P(None, None, "blk"), check_vma=False
    )
```

profile of v0, /device:TPU:16, one launch (start us, length us, event | category | flops | bytes accessed | tf_op | source)
XLA Modules:
  0.0 537.4 jit_solution(5126460402475514423)
XLA Ops:
  7.5 1.8 copy_multiply_fusion
  10.6 4.5 collective-permute-start
  15.2 1.3 collective-permute-done
  18.8 4.5 collective-permute-start.2
  23.4 1.3 collective-permute-done.2
  27.1 1.9 broadcast_multiply_fusion
  30.3 4.8 collective-permute-start.4
  35.2 1.3 collective-permute-done.4
  37.6 1.4 copy.13
  40.6 4.8 collective-permute-start.6
  49.2 2.6 fusion.34
  53.1 4.8 collective-permute-start.8
  58.0 1.3 collective-permute-done.8
  60.4 1.4 copy.17
  61.8 5.0 collective-permute-start.10
  68.8 5.0 collective-permute-done.11
  75.0 1.8 fusion.27
  78.1 4.9 collective-permute-start.12
  83.1 1.3 collective-permute-done.12
  85.5 1.4 copy.21
  88.5 5.4 %collective-permute-start.14 = (f32[8,130,1]{1,0,2:T(8,128)S(1)}, f32[8,130,1]{1,0,2:T(8,128)S(1)}, u32[]{:S(2)}, u32[]{:S(2)}) collective-permute-start(f32[8,130,1]{1,0,2:T(8,128)S(1)} %copy.21), channel_id=1, source_target_pairs={{0,4},{4,8},{8,12},{12,16},{16,20},{20,24},{24,28},{1,5},{5,9},{9,... | collective-permute-start | bytes 12488 | tf_op jit(solution)/shard_map/ppermute | solution.py:13
  97.7 8.3 %fusion.20 = f32[8,128,256]{2,0,1:T(8,128)S(1)} fusion(f32[8,128,256]{2,0,1:T(8,128)S(1)} %fusion.34, f32[8,128,256]{2,0,1:T(8,128)} %copy-done, f32[8,1,256]{2,0,1:T(8,128)S(1)} %collective-permute-done.12, f32[8,1,256]{2,0,1:T(8,128)S(1)} %collective-permute-done.13, f32[8,130,1]{2,0,1:T(8,128)} %copy.24, f32[8,130,1]{2,0,1:T(8,128)} %copy.22, ...), kind=kLoop, calls=%fused_computation.33 | loop fusion | flops 6815744 | bytes 5562516 | tf_op jit(solution)/shard_map/add | solution.py:60
  107.3 6.0 %collective-permute-start.16 = (f32[8,1,256]{2,0,1:T(8,128)S(1)}, f32[8,1,256]{2,0,1:T(8,128)S(1)}, u32[]{:S(2)}, u32[]{:S(2)}) collective-permute-start(f32[8,1,256]{2,0,1:T(8,128)S(1)} %get-tuple-element.18), channel_id=1, source_target_pairs={{0,32},{32,64},{64,96},{96,128},{128,160},{160,192},{192,224},{1,3... | collective-permute-start | bytes 24584 | tf_op jit(solution)/shard_map/ppermute | solution.py:13
  113.3 1.3 collective-permute-done.16
  115.3 4.8 collective-permute-start.18
  120.5 1.5 collective-permute-start.19
  122.4 4.8 collective-permute-done.19
  128.4 1.8 fusion.11
  130.2 1.5 pad_maximum_fusion
  131.7 71.7 %all-gather.2.cloned.1.call-done = f32[2,32,128,256]{3,1,2,0:T(8,128)} async-done(((f32[2,8,128,256]{3,1,2,0:T(8,128)}), f32[2,32,128,256]{3,1,2,0:T(8,128)}) %all-gather.2.cloned.1.call-update) | async-done | bytes 8388624 | tf_op jit(solution)/shard_map/all_gather | solution.py:66
  203.4 16.7 %fusion.3 = f32[2,32,64]{2,1,0:T(8,128)S(1)} fusion(f32[2,32,128,256]{3,1,2,0:T(8,128)} %all-gather.2.cloned.1.call-done, f32[64,128,256]{2,1,0:T(8,128)} %param.6), kind=kOutput, calls=%fused_computation.4 | convolution fusion | flops 1610612736 | bytes 16793600 | tf_op jit(solution)/shard_map/dot_general | solution.py:39
  220.0 309.9 %psum.7 = f32[2,32,64]{2,1,0:T(8,128)S(1)} all-reduce(f32[2,32,64]{2,1,0:T(8,128)S(1)} %fusion.3), channel_id=1, replica_groups=mesh['lx'=8,'ly'=8,'blk'=4] {'lx','ly'}, use_global_device_ids=true, to_apply=%region_0.1 | all-reduce | flops 4096 | bytes 32768 | tf_op jit(solution)/shard_map/psum | solution.py:67
  (66 shorter events, 31.8 us)
Async XLA Ops:
  6.5 196.8 %all-gather.2.cloned.1.call-start = ((), (), s32[]{:S(2)}) async-start(), calls=%async_computation | async-start | bytes 10485760 | tf_op jit(solution)/shard_map/all_gather | solution.py:66
  9.3 5.9 %collective-permute-start.1 = (f32[8,1,256]{2,0,1:T(8,128)S(1)}, f32[8,1,256]{2,0,1:T(8,128)S(1)}, u32[]{:S(2)}, u32[]{:S(2)}) collective-permute-start(f32[8,1,256]{2,0,1:T(8,128)S(1)} %get-tuple-element.25), channel_id=1, source_target_pairs={{32,0},{64,32},{96,64},{128,96},{160,128},{192,160},{224,192},{33,... | collective-permute-start | bytes 24584 | tf_op jit(solution)/shard_map/ppermute | solution.py:16
  10.6 5.9 %collective-permute-start = (f32[8,1,256]{2,0,1:T(8,128)S(1)}, f32[8,1,256]{2,0,1:T(8,128)S(1)}, u32[]{:S(2)}, u32[]{:S(2)}) collective-permute-start(f32[8,1,256]{2,0,1:T(8,128)S(1)} %get-tuple-element.26), channel_id=1, source_target_pairs={{0,32},{32,64},{64,96},{96,128},{128,160},{160,192},{192,224},{1,3... | collective-permute-start | bytes 24584 | tf_op jit(solution)/shard_map/ppermute | solution.py:13
  16.8 10.3 %copy-start.1 = (f32[128,256]{1,0:T(8,128)S(1)}, f32[128,256]{1,0:T(8,128)}, u32[]{:S(2)}) copy-start(f32[128,256]{1,0:T(8,128)} %param.7) | copy-start | bytes 393220
  17.5 8.4 %collective-permute-start.3 = (f32[8,130,1]{1,0,2:T(8,128)S(1)}, f32[8,130,1]{1,0,2:T(8,128)S(1)}, u32[]{:S(2)}, u32[]{:S(2)}) collective-permute-start(f32[8,130,1]{1,0,2:T(8,128)S(1)} %copy.11), channel_id=1, source_target_pairs={{4,0},{8,4},{12,8},{16,12},{20,16},{24,20},{28,24},{5,1},{9,5},{13... | collective-permute-start | bytes 12488 | tf_op jit(solution)/shard_map/ppermute | solution.py:16
  18.8 5.9 %collective-permute-start.2 = (f32[8,130,1]{1,0,2:T(8,128)S(1)}, f32[8,130,1]{1,0,2:T(8,128)S(1)}, u32[]{:S(2)}, u32[]{:S(2)}) collective-permute-start(f32[8,130,1]{1,0,2:T(8,128)S(1)} %copy.9), channel_id=1, source_target_pairs={{0,4},{4,8},{8,12},{12,16},{16,20},{20,24},{24,28},{1,5},{5,9},{9,... | collective-permute-start | bytes 12488 | tf_op jit(solution)/shard_map/ppermute | solution.py:13
  29.0 6.1 %collective-permute-start.5 = (f32[8,1,256]{2,0,1:T(8,128)S(1)}, f32[8,1,256]{2,0,1:T(8,128)S(1)}, u32[]{:S(2)}, u32[]{:S(2)}) collective-permute-start(f32[8,1,256]{2,0,1:T(8,128)S(1)} %get-tuple-element.23), channel_id=1, source_target_pairs={{32,0},{64,32},{96,64},{128,96},{160,128},{192,160},{224,192},{33,... | collective-permute-start | bytes 24584 | tf_op jit(solution)/shard_map/ppermute | solution.py:16
  30.3 6.2 %collective-permute-start.4 = (f32[8,1,256]{2,0,1:T(8,128)S(1)}, f32[8,1,256]{2,0,1:T(8,128)S(1)}, u32[]{:S(2)}, u32[]{:S(2)}) collective-permute-start(f32[8,1,256]{2,0,1:T(8,128)S(1)} %get-tuple-element.24), channel_id=1, source_target_pairs={{0,32},{32,64},{64,96},{96,128},{128,160},{160,192},{192,224},{1,3... | collective-permute-start | bytes 24584 | tf_op jit(solution)/shard_map/ppermute | solution.py:13
  39.3 8.7 %collective-permute-start.7 = (f32[8,130,1]{1,0,2:T(8,128)S(1)}, f32[8,130,1]{1,0,2:T(8,128)S(1)}, u32[]{:S(2)}, u32[]{:S(2)}) collective-permute-start(f32[8,130,1]{1,0,2:T(8,128)S(1)} %copy.15), channel_id=1, source_target_pairs={{4,0},{8,4},{12,8},{16,12},{20,16},{24,20},{28,24},{5,1},{9,5},{13... | collective-permute-start | bytes 12488 | tf_op jit(solution)/shard_map/ppermute | solution.py:16
  40.6 6.2 %collective-permute-start.6 = (f32[8,130,1]{1,0,2:T(8,128)S(1)}, f32[8,130,1]{1,0,2:T(8,128)S(1)}, u32[]{:S(2)}, u32[]{:S(2)}) collective-permute-start(f32[8,130,1]{1,0,2:T(8,128)S(1)} %copy.13), channel_id=1, source_target_pairs={{0,4},{4,8},{8,12},{12,16},{16,20},{20,24},{24,28},{1,5},{5,9},{9,... | collective-permute-start | bytes 12488 | tf_op jit(solution)/shard_map/ppermute | solution.py:13
  51.8 6.1 %collective-permute-start.9 = (f32[8,1,256]{2,0,1:T(8,128)S(1)}, f32[8,1,256]{2,0,1:T(8,128)S(1)}, u32[]{:S(2)}, u32[]{:S(2)}) collective-permute-start(f32[8,1,256]{2,0,1:T(8,128)S(1)} %get-tuple-element.21), channel_id=1, source_target_pairs={{32,0},{64,32},{96,64},{128,96},{160,128},{192,160},{224,192},{33,... | collective-permute-start | bytes 24584 | tf_op jit(solution)/shard_map/ppermute | solution.py:16
  53.1 6.2 %collective-permute-start.8 = (f32[8,1,256]{2,0,1:T(8,128)S(1)}, f32[8,1,256]{2,0,1:T(8,128)S(1)}, u32[]{:S(2)}, u32[]{:S(2)}) collective-permute-start(f32[8,1,256]{2,0,1:T(8,128)S(1)} %get-tuple-element.22), channel_id=1, source_target_pairs={{0,32},{32,64},{64,96},{96,128},{128,160},{160,192},{192,224},{1,3... | collective-permute-start | bytes 24584 | tf_op jit(solution)/shard_map/ppermute | solution.py:13
  61.8 6.6 %collective-permute-start.10 = (f32[8,130,1]{1,0,2:T(8,128)S(1)}, f32[8,130,1]{1,0,2:T(8,128)S(1)}, u32[]{:S(2)}, u32[]{:S(2)}) collective-permute-start(f32[8,130,1]{1,0,2:T(8,128)S(1)} %copy.17), channel_id=1, source_target_pairs={{0,4},{4,8},{8,12},{12,16},{16,20},{20,24},{24,28},{1,5},{5,9},{9,... | collective-permute-start | bytes 12488 | tf_op jit(solution)/shard_map/ppermute | solution.py:13
  67.1 6.7 %collective-permute-start.11 = (f32[8,130,1]{1,0,2:T(8,128)S(1)}, f32[8,130,1]{1,0,2:T(8,128)S(1)}, u32[]{:S(2)}, u32[]{:S(2)}) collective-permute-start(f32[8,130,1]{1,0,2:T(8,128)S(1)} %copy.19), channel_id=1, source_target_pairs={{4,0},{8,4},{12,8},{16,12},{20,16},{24,20},{28,24},{5,1},{9,5},{13... | collective-permute-start | bytes 12488 | tf_op jit(solution)/shard_map/ppermute | solution.py:16
  76.8 7.7 %copy-start = (f32[8,128,256]{2,0,1:T(8,128)}, f32[8,128,256]{2,0,1:T(8,128)S(1)}, u32[]{:S(2)}) copy-start(f32[8,128,256]{2,0,1:T(8,128)S(1)} %fusion.27) | copy-start | bytes 3145732
  76.8 6.2 %collective-permute-start.13 = (f32[8,1,256]{2,0,1:T(8,128)S(1)}, f32[8,1,256]{2,0,1:T(8,128)S(1)}, u32[]{:S(2)}, u32[]{:S(2)}) collective-permute-start(f32[8,1,256]{2,0,1:T(8,128)S(1)} %get-tuple-element.19), channel_id=1, source_target_pairs={{32,0},{64,32},{96,64},{128,96},{160,128},{192,160},{224,192},{33,... | collective-permute-start | bytes 24584 | tf_op jit(solution)/shard_map/ppermute | solution.py:16
  78.1 6.3 %collective-permute-start.12 = (f32[8,1,256]{2,0,1:T(8,128)S(1)}, f32[8,1,256]{2,0,1:T(8,128)S(1)}, u32[]{:S(2)}, u32[]{:S(2)}) collective-permute-start(f32[8,1,256]{2,0,1:T(8,128)S(1)} %get-tuple-element.20), channel_id=1, source_target_pairs={{0,32},{32,64},{64,96},{96,128},{128,160},{160,192},{192,224},{1,3... | collective-permute-start | bytes 24584 | tf_op jit(solution)/shard_map/ppermute | solution.py:13
  85.5 8.5 %copy-start.2 = (f32[5]{0:T(128)S(1)}, f32[5]{0:T(128)}, u32[]{:S(2)}) copy-start(f32[5]{0:T(128)} %param.9) | copy-start | bytes 64
  87.2 9.3 %collective-permute-start.15 = (f32[8,130,1]{1,0,2:T(8,128)S(1)}, f32[8,130,1]{1,0,2:T(8,128)S(1)}, u32[]{:S(2)}, u32[]{:S(2)}) collective-permute-start(f32[8,130,1]{1,0,2:T(8,128)S(1)} %copy.23), channel_id=1, source_target_pairs={{4,0},{8,4},{12,8},{16,12},{20,16},{24,20},{28,24},{5,1},{9,5},{13... | collective-permute-start | bytes 12488 | tf_op jit(solution)/shard_map/ppermute | solution.py:16
  88.5 6.8 %collective-permute-start.14 = (f32[8,130,1]{1,0,2:T(8,128)S(1)}, f32[8,130,1]{1,0,2:T(8,128)S(1)}, u32[]{:S(2)}, u32[]{:S(2)}) collective-permute-start(f32[8,130,1]{1,0,2:T(8,128)S(1)} %copy.21), channel_id=1, source_target_pairs={{0,4},{4,8},{8,12},{12,16},{16,20},{20,24},{24,28},{1,5},{5,9},{9,... | collective-permute-start | bytes 12488 | tf_op jit(solution)/shard_map/ppermute | solution.py:13
  106.0 7.3 %collective-permute-start.17 = (f32[8,1,256]{2,0,1:T(8,128)S(1)}, f32[8,1,256]{2,0,1:T(8,128)S(1)}, u32[]{:S(2)}, u32[]{:S(2)}) collective-permute-start(f32[8,1,256]{2,0,1:T(8,128)S(1)} %get-tuple-element.17), channel_id=1, source_target_pairs={{32,0},{64,32},{96,64},{128,96},{160,128},{192,160},{224,192},{33,... | collective-permute-start | bytes 24584 | tf_op jit(solution)/shard_map/ppermute | solution.py:16
  107.3 7.4 %collective-permute-start.16 = (f32[8,1,256]{2,0,1:T(8,128)S(1)}, f32[8,1,256]{2,0,1:T(8,128)S(1)}, u32[]{:S(2)}, u32[]{:S(2)}) collective-permute-start(f32[8,1,256]{2,0,1:T(8,128)S(1)} %get-tuple-element.18), channel_id=1, source_target_pairs={{0,32},{32,64},{64,96},{96,128},{128,160},{160,192},{192,224},{1,3... | collective-permute-start | bytes 24584 | tf_op jit(solution)/shard_map/ppermute | solution.py:13
  115.3 6.7 %collective-permute-start.18 = (f32[8,130,1]{1,0,2:T(8,128)S(1)}, f32[8,130,1]{1,0,2:T(8,128)S(1)}, u32[]{:S(2)}, u32[]{:S(2)}) collective-permute-start(f32[8,130,1]{1,0,2:T(8,128)S(1)} %copy.25), channel_id=1, source_target_pairs={{0,4},{4,8},{8,12},{12,16},{16,20},{20,24},{24,28},{1,5},{5,9},{9,... | collective-permute-start | bytes 12488 | tf_op jit(solution)/shard_map/ppermute | solution.py:13
  120.5 6.7 %collective-permute-start.19 = (f32[8,130,1]{1,0,2:T(8,128)S(1)}, f32[8,130,1]{1,0,2:T(8,128)S(1)}, u32[]{:S(2)}, u32[]{:S(2)}) collective-permute-start(f32[8,130,1]{1,0,2:T(8,128)S(1)} %copy.27), channel_id=1, source_target_pairs={{4,0},{8,4},{12,8},{16,12},{20,16},{24,20},{28,24},{5,1},{9,5},{13... | collective-permute-start | bytes 12488 | tf_op jit(solution)/shard_map/ppermute | solution.py:16
Sparse Core Ops, SparseCore 0:
  131.8 71.4 all-gather.1
where the time goes:
time: 538 us; the launch traced here: 537 us
  blocking collectives  310 us (58%)
  waiting for transfers between devices  90.3 us (17%)
  starting transfers between devices  62.9 us (12%)
  other arithmetic  22.4 us (4%)
  local copies, waits for them, and re-layouts  20.9 us (4%)
  matrix products  16.7 us (3%)
  between operations  14.3 us (3%)
    psum x1, blocking collectives, shards(): total = lax.psum(partial_gram, ('lx', 'ly'))  310 us
    all_gather x1, waiting for transfers between devices, shards(): lax.all_gather(paired, 'blk', axis=1, tiled=True)  71.7 us
    ppermute x10, starting transfers between devices, extended(): lax.ppermute(lax.slice_in_dim(block, block.shape[dim] - width, None, axis...  49.7 us
    dot_general x1, matrix products, gram_rows(): lax.dot_general(flat, search_flat, (((1,), (1,)), ((), ())), precision=la...  16.7 us
    ppermute x10, starting transfers between devices, extended(): lax.ppermute(lax.slice_in_dim(block, 0, width, axis=dim), axis, backward)  13.1 us
  transfers between devices with their start and end apart: 21, of which 11 were waited for; matrix products, arithmetic and copies ran while one was open for 1% of the time, Pallas kernels for 0%

commit v1 on v0

--- a/solution.py
+++ b/solution.py
@@ -64,7 +64,10 @@
     image = scaled_step(padded_field, onsite_energy, present)
     paired = jnp.stack([filtered, image])
     partial_gram = gram_rows(lax.all_gather(paired, "blk", axis=1, tiled=True), search_vectors)
-    total = lax.psum(partial_gram, ("lx", "ly"))
+    case_cut = lambda patch, comm_axis, mesh_ax: lax.psum(
+        lax.psum(patch, axis_name=comm_axis), mesh_ax
+    )
+    total = case_cut(partial_gram, "ly", mesh_ax="lx")
     return total * scale_factor
 
 

time: 538 us -> 294 us (0.55)
  blocking collectives: 310 us -> 65.1 us
    psum x1 -> x2, blocking collectives: 310 us -> 65.1 us  [the longest x1 34.9 us: shards(): lax.psum(patch, axis_name=comm_axis)]
  transfers between devices with their start and end apart: 21 -> 21, of which waited for: 11 -> 10; matrix products, arithmetic and copies ran while one was open for 1% -> 2% of each run, Pallas kernels for 0% -> 0%
where the time goes in v1:
time: 294 us; the launch traced here: 293 us
  waiting for transfers between devices  90.2 us (31%)
  blocking collectives  65.1 us (22%)
  starting transfers between devices  62.9 us (21%)
  other arithmetic  22.4 us (8%)
  local copies, waits for them, and re-layouts  21 us (7%)
  matrix products  16.7 us (6%)
  between operations  14.4 us (5%)
    all_gather x1, waiting for transfers between devices, shards(): lax.all_gather(paired, 'blk', axis=1, tiled=True)  71.7 us
    ppermute x10, starting transfers between devices, extended(): lax.ppermute(lax.slice_in_dim(block, block.shape[dim] - width, None, axis...  49.7 us
    psum x1, blocking collectives, shards(): lax.psum(patch, axis_name=comm_axis)  34.9 us
    psum x1, blocking collectives, shards(): lax.psum(lax.psum(patch, axis_name=comm_axis), mesh_ax)  30.2 us
    dot_general x1, matrix products, gram_rows(): lax.dot_general(flat, search_flat, (((1,), (1,)), ((), ())), precision=la...  16.7 us
    ppermute x10, starting transfers between devices, extended(): lax.ppermute(lax.slice_in_dim(block, 0, width, axis=dim), axis, backward)  13.1 us
    ppermute x10, waiting for transfers between devices, extended(): lax.ppermute(lax.slice_in_dim(block, 0, width, axis=dim), axis, backward)  9.85 us
    ppermute x10, waiting for transfers between devices, extended(): lax.ppermute(lax.slice_in_dim(block, block.shape[dim] - width, None, axis...  8.71 us
  transfers between devices with their start and end apart: 21, of which 10 were waited for; matrix products, arithmetic and copies ran while one was open for 2% of the time, Pallas kernels for 0%

profile of v1, /device:TPU:16, one launch (start us, length us, event | category | flops | bytes accessed | tf_op | source)
XLA Modules:
  0.0 292.8 jit_solution(8926001301729085874)
XLA Ops:
  7.5 1.8 copy_multiply_fusion
  10.6 4.5 %collective-permute-start = (f32[8,1,256]{2,0,1:T(8,128)S(1)}, f32[8,1,256]{2,0,1:T(8,128)S(1)}, u32[]{:S(2)}, u32[]{:S(2)}) collective-permute-start(f32[8,1,256]{2,0,1:T(8,128)S(1)} %get-tuple-element.26), channel_id=1, source_target_pairs={{0,32},{32,64},{64,96},{96,128},{128,160},{160,192},{192,224},{1,3... | collective-permute-start | bytes 24584 | tf_op jit(solution)/shard_map/ppermute | solution.py:13
  15.2 1.3 collective-permute-done
  18.8 4.5 %collective-permute-start.2 = (f32[8,130,1]{1,0,2:T(8,128)S(1)}, f32[8,130,1]{1,0,2:T(8,128)S(1)}, u32[]{:S(2)}, u32[]{:S(2)}) collective-permute-start(f32[8,130,1]{1,0,2:T(8,128)S(1)} %copy.9), channel_id=1, source_target_pairs={{0,4},{4,8},{8,12},{12,16},{16,20},{20,24},{24,28},{1,5},{5,9},{9,... | collective-permute-start | bytes 12488 | tf_op jit(solution)/shard_map/ppermute | solution.py:13
  27.1 1.9 broadcast_multiply_fusion
  30.4 4.8 %collective-permute-start.4 = (f32[8,1,256]{2,0,1:T(8,128)S(1)}, f32[8,1,256]{2,0,1:T(8,128)S(1)}, u32[]{:S(2)}, u32[]{:S(2)}) collective-permute-start(f32[8,1,256]{2,0,1:T(8,128)S(1)} %get-tuple-element.24), channel_id=1, source_target_pairs={{0,32},{32,64},{64,96},{96,128},{128,160},{160,192},{192,224},{1,3... | collective-permute-start | bytes 24584 | tf_op jit(solution)/shard_map/ppermute | solution.py:13
  35.2 1.3 collective-permute-done.4
  37.6 1.4 copy.13
  40.7 4.8 %collective-permute-start.6 = (f32[8,130,1]{1,0,2:T(8,128)S(1)}, f32[8,130,1]{1,0,2:T(8,128)S(1)}, u32[]{:S(2)}, u32[]{:S(2)}) collective-permute-start(f32[8,130,1]{1,0,2:T(8,128)S(1)} %copy.13), channel_id=1, source_target_pairs={{0,4},{4,8},{8,12},{12,16},{16,20},{20,24},{24,28},{1,5},{5,9},{9,... | collective-permute-start | bytes 12488 | tf_op jit(solution)/shard_map/ppermute | solution.py:13
  49.2 2.6 fusion.34
  53.1 4.8 %collective-permute-start.8 = (f32[8,1,256]{2,0,1:T(8,128)S(1)}, f32[8,1,256]{2,0,1:T(8,128)S(1)}, u32[]{:S(2)}, u32[]{:S(2)}) collective-permute-start(f32[8,1,256]{2,0,1:T(8,128)S(1)} %get-tuple-element.22), channel_id=1, source_target_pairs={{0,32},{32,64},{64,96},{96,128},{128,160},{160,192},{192,224},{1,3... | collective-permute-start | bytes 24584 | tf_op jit(solution)/shard_map/ppermute | solution.py:13
  58.0 1.3 collective-permute-done.8
  60.4 1.4 copy.17
  61.8 5.0 %collective-permute-start.10 = (f32[8,130,1]{1,0,2:T(8,128)S(1)}, f32[8,130,1]{1,0,2:T(8,128)S(1)}, u32[]{:S(2)}, u32[]{:S(2)}) collective-permute-start(f32[8,130,1]{1,0,2:T(8,128)S(1)} %copy.17), channel_id=1, source_target_pairs={{0,4},{4,8},{8,12},{12,16},{16,20},{20,24},{24,28},{1,5},{5,9},{9,... | collective-permute-start | bytes 12488 | tf_op jit(solution)/shard_map/ppermute | solution.py:13
  68.8 5.0 %collective-permute-done.11 = f32[8,130,1]{1,0,2:T(8,128)S(1)} collective-permute-done((f32[8,130,1]{1,0,2:T(8,128)S(1)}, f32[8,130,1]{1,0,2:T(8,128)S(1)}, u32[]{:S(2)}, u32[]{:S(2)}) %collective-permute-start.11) | collective-permute-done | bytes 4192 | tf_op jit(solution)/shard_map/ppermute | solution.py:16
  75.0 1.8 fusion.27
  78.2 4.9 %collective-permute-start.12 = (f32[8,1,256]{2,0,1:T(8,128)S(1)}, f32[8,1,256]{2,0,1:T(8,128)S(1)}, u32[]{:S(2)}, u32[]{:S(2)}) collective-permute-start(f32[8,1,256]{2,0,1:T(8,128)S(1)} %get-tuple-element.20), channel_id=1, source_target_pairs={{0,32},{32,64},{64,96},{96,128},{128,160},{160,192},{192,224},{1,3... | collective-permute-start | bytes 24584 | tf_op jit(solution)/shard_map/ppermute | solution.py:13
  83.1 1.3 collective-permute-done.12
  85.5 1.4 copy.21
  88.6 5.4 %collective-permute-start.14 = (f32[8,130,1]{1,0,2:T(8,128)S(1)}, f32[8,130,1]{1,0,2:T(8,128)S(1)}, u32[]{:S(2)}, u32[]{:S(2)}) collective-permute-start(f32[8,130,1]{1,0,2:T(8,128)S(1)} %copy.21), channel_id=1, source_target_pairs={{0,4},{4,8},{8,12},{12,16},{16,20},{20,24},{24,28},{1,5},{5,9},{9,... | collective-permute-start | bytes 12488 | tf_op jit(solution)/shard_map/ppermute | solution.py:13
  97.7 8.3 %fusion.20 = f32[8,128,256]{2,0,1:T(8,128)S(1)} fusion(f32[8,128,256]{2,0,1:T(8,128)S(1)} %fusion.34, f32[8,128,256]{2,0,1:T(8,128)} %copy-done, f32[8,1,256]{2,0,1:T(8,128)S(1)} %collective-permute-done.12, f32[8,1,256]{2,0,1:T(8,128)S(1)} %collective-permute-done.13, f32[8,130,1]{2,0,1:T(8,128)} %copy.24, f32[8,130,1]{2,0,1:T(8,128)} %copy.22, ...), kind=kLoop, calls=%fused_computation.33 | loop fusion | flops 6815744 | bytes 5562516 | tf_op jit(solution)/shard_map/add | solution.py:60
  107.4 6.0 %collective-permute-start.16 = (f32[8,1,256]{2,0,1:T(8,128)S(1)}, f32[8,1,256]{2,0,1:T(8,128)S(1)}, u32[]{:S(2)}, u32[]{:S(2)}) collective-permute-start(f32[8,1,256]{2,0,1:T(8,128)S(1)} %get-tuple-element.18), channel_id=1, source_target_pairs={{0,32},{32,64},{64,96},{96,128},{128,160},{160,192},{192,224},{1,3... | collective-permute-start | bytes 24584 | tf_op jit(solution)/shard_map/ppermute | solution.py:13
  113.5 1.3 collective-permute-done.16
  115.4 4.8 %collective-permute-start.18 = (f32[8,130,1]{1,0,2:T(8,128)S(1)}, f32[8,130,1]{1,0,2:T(8,128)S(1)}, u32[]{:S(2)}, u32[]{:S(2)}) collective-permute-start(f32[8,130,1]{1,0,2:T(8,128)S(1)} %copy.25), channel_id=1, source_target_pairs={{0,4},{4,8},{8,12},{12,16},{16,20},{20,24},{24,28},{1,5},{5,9},{9,... | collective-permute-start | bytes 12488 | tf_op jit(solution)/shard_map/ppermute | solution.py:13
  120.6 1.5 collective-permute-start.19
  122.5 4.8 %collective-permute-done.19 = f32[8,130,1]{1,0,2:T(8,128)S(1)} collective-permute-done((f32[8,130,1]{1,0,2:T(8,128)S(1)}, f32[8,130,1]{1,0,2:T(8,128)S(1)}, u32[]{:S(2)}, u32[]{:S(2)}) %collective-permute-start.19) | collective-permute-done | bytes 4192 | tf_op jit(solution)/shard_map/ppermute | solution.py:16
  128.5 1.8 fusion.11
  130.3 1.5 pad_maximum_fusion
  131.8 71.7 %all-gather.2.cloned.1.call-done = f32[2,32,128,256]{3,1,2,0:T(8,128)} async-done(((f32[2,8,128,256]{3,1,2,0:T(8,128)}), f32[2,32,128,256]{3,1,2,0:T(8,128)}) %all-gather.2.cloned.1.call-update) | async-done | bytes 8388624 | tf_op jit(solution)/shard_map/all_gather | solution.py:66
  203.5 16.7 %fusion.3 = f32[2,32,64]{2,1,0:T(8,128)S(1)} fusion(f32[2,32,128,256]{3,1,2,0:T(8,128)} %all-gather.2.cloned.1.call-done, f32[64,128,256]{2,1,0:T(8,128)} %param.6), kind=kOutput, calls=%fused_computation.4 | convolution fusion | flops 1610612736 | bytes 16793600 | tf_op jit(solution)/shard_map/dot_general | solution.py:39
  220.2 34.9 %psum.14 = f32[2,32,64]{2,1,0:T(8,128)S(1)} all-reduce(f32[2,32,64]{2,1,0:T(8,128)S(1)} %fusion.3), channel_id=1, replica_groups=mesh['lx'=8,'ly'=8,'blk'=4] {'ly'}, use_global_device_ids=true, to_apply=%region_0.1 | all-reduce | flops 4096 | bytes 32768 | tf_op jit(solution)/shard_map/psum | solution.py:68
  255.1 30.2 %psum.15 = f32[2,32,64]{2,1,0:T(8,128)S(1)} all-reduce(f32[2,32,64]{2,1,0:T(8,128)S(1)} %psum.14), channel_id=1, replica_groups=mesh['lx'=8,'ly'=8,'blk'=4] {'lx'}, use_global_device_ids=true, to_apply=%region_1.2 | all-reduce | flops 4096 | bytes 32768 | tf_op jit(solution)/shard_map/psum | solution.py:67
  (67 shorter events, 33.1 us)
Async XLA Ops:
  6.5 197.0 %all-gather.2.cloned.1.call-start = ((), (), s32[]{:S(2)}) async-start(), calls=%async_computation | async-start | bytes 10485760 | tf_op jit(solution)/shard_map/all_gather | solution.py:66
  9.3 5.9 %collective-permute-start.1 = (f32[8,1,256]{2,0,1:T(8,128)S(1)}, f32[8,1,256]{2,0,1:T(8,128)S(1)}, u32[]{:S(2)}, u32[]{:S(2)}) collective-permute-start(f32[8,1,256]{2,0,1:T(8,128)S(1)} %get-tuple-element.25), channel_id=1, source_target_pairs={{32,0},{64,32},{96,64},{128,96},{160,128},{192,160},{224,192},{33,... | collective-permute-start | bytes 24584 | tf_op jit(solution)/shard_map/ppermute | solution.py:16
  10.6 5.9 %collective-permute-start = (f32[8,1,256]{2,0,1:T(8,128)S(1)}, f32[8,1,256]{2,0,1:T(8,128)S(1)}, u32[]{:S(2)}, u32[]{:S(2)}) collective-permute-start(f32[8,1,256]{2,0,1:T(8,128)S(1)} %get-tuple-element.26), channel_id=1, source_target_pairs={{0,32},{32,64},{64,96},{96,128},{128,160},{160,192},{192,224},{1,3... | collective-permute-start | bytes 24584 | tf_op jit(solution)/shard_map/ppermute | solution.py:13
  16.8 10.3 %copy-start.1 = (f32[128,256]{1,0:T(8,128)S(1)}, f32[128,256]{1,0:T(8,128)}, u32[]{:S(2)}) copy-start(f32[128,256]{1,0:T(8,128)} %param.7) | copy-start | bytes 393220
  17.5 8.4 %collective-permute-start.3 = (f32[8,130,1]{1,0,2:T(8,128)S(1)}, f32[8,130,1]{1,0,2:T(8,128)S(1)}, u32[]{:S(2)}, u32[]{:S(2)}) collective-permute-start(f32[8,130,1]{1,0,2:T(8,128)S(1)} %copy.11), channel_id=1, source_target_pairs={{4,0},{8,4},{12,8},{16,12},{20,16},{24,20},{28,24},{5,1},{9,5},{13... | collective-permute-start | bytes 12488 | tf_op jit(solution)/shard_map/ppermute | solution.py:16
  18.8 5.9 %collective-permute-start.2 = (f32[8,130,1]{1,0,2:T(8,128)S(1)}, f32[8,130,1]{1,0,2:T(8,128)S(1)}, u32[]{:S(2)}, u32[]{:S(2)}) collective-permute-start(f32[8,130,1]{1,0,2:T(8,128)S(1)} %copy.9), channel_id=1, source_target_pairs={{0,4},{4,8},{8,12},{12,16},{16,20},{20,24},{24,28},{1,5},{5,9},{9,... | collective-permute-start | bytes 12488 | tf_op jit(solution)/shard_map/ppermute | solution.py:13
  29.1 6.1 %collective-permute-start.5 = (f32[8,1,256]{2,0,1:T(8,128)S(1)}, f32[8,1,256]{2,0,1:T(8,128)S(1)}, u32[]{:S(2)}, u32[]{:S(2)}) collective-permute-start(f32[8,1,256]{2,0,1:T(8,128)S(1)} %get-tuple-element.23), channel_id=1, source_target_pairs={{32,0},{64,32},{96,64},{128,96},{160,128},{192,160},{224,192},{33,... | collective-permute-start | bytes 24584 | tf_op jit(solution)/shard_map/ppermute | solution.py:16
  30.4 6.2 %collective-permute-start.4 = (f32[8,1,256]{2,0,1:T(8,128)S(1)}, f32[8,1,256]{2,0,1:T(8,128)S(1)}, u32[]{:S(2)}, u32[]{:S(2)}) collective-permute-start(f32[8,1,256]{2,0,1:T(8,128)S(1)} %get-tuple-element.24), channel_id=1, source_target_pairs={{0,32},{32,64},{64,96},{96,128},{128,160},{160,192},{192,224},{1,3... | collective-permute-start | bytes 24584 | tf_op jit(solution)/shard_map/ppermute | solution.py:13
  39.4 8.7 %collective-permute-start.7 = (f32[8,130,1]{1,0,2:T(8,128)S(1)}, f32[8,130,1]{1,0,2:T(8,128)S(1)}, u32[]{:S(2)}, u32[]{:S(2)}) collective-permute-start(f32[8,130,1]{1,0,2:T(8,128)S(1)} %copy.15), channel_id=1, source_target_pairs={{4,0},{8,4},{12,8},{16,12},{20,16},{24,20},{28,24},{5,1},{9,5},{13... | collective-permute-start | bytes 12488 | tf_op jit(solution)/shard_map/ppermute | solution.py:16
  40.7 6.2 %collective-permute-start.6 = (f32[8,130,1]{1,0,2:T(8,128)S(1)}, f32[8,130,1]{1,0,2:T(8,128)S(1)}, u32[]{:S(2)}, u32[]{:S(2)}) collective-permute-start(f32[8,130,1]{1,0,2:T(8,128)S(1)} %copy.13), channel_id=1, source_target_pairs={{0,4},{4,8},{8,12},{12,16},{16,20},{20,24},{24,28},{1,5},{5,9},{9,... | collective-permute-start | bytes 12488 | tf_op jit(solution)/shard_map/ppermute | solution.py:13
  51.8 6.1 %collective-permute-start.9 = (f32[8,1,256]{2,0,1:T(8,128)S(1)}, f32[8,1,256]{2,0,1:T(8,128)S(1)}, u32[]{:S(2)}, u32[]{:S(2)}) collective-permute-start(f32[8,1,256]{2,0,1:T(8,128)S(1)} %get-tuple-element.21), channel_id=1, source_target_pairs={{32,0},{64,32},{96,64},{128,96},{160,128},{192,160},{224,192},{33,... | collective-permute-start | bytes 24584 | tf_op jit(solution)/shard_map/ppermute | solution.py:16
  53.1 6.2 %collective-permute-start.8 = (f32[8,1,256]{2,0,1:T(8,128)S(1)}, f32[8,1,256]{2,0,1:T(8,128)S(1)}, u32[]{:S(2)}, u32[]{:S(2)}) collective-permute-start(f32[8,1,256]{2,0,1:T(8,128)S(1)} %get-tuple-element.22), channel_id=1, source_target_pairs={{0,32},{32,64},{64,96},{96,128},{128,160},{160,192},{192,224},{1,3... | collective-permute-start | bytes 24584 | tf_op jit(solution)/shard_map/ppermute | solution.py:13
  61.8 6.6 %collective-permute-start.10 = (f32[8,130,1]{1,0,2:T(8,128)S(1)}, f32[8,130,1]{1,0,2:T(8,128)S(1)}, u32[]{:S(2)}, u32[]{:S(2)}) collective-permute-start(f32[8,130,1]{1,0,2:T(8,128)S(1)} %copy.17), channel_id=1, source_target_pairs={{0,4},{4,8},{8,12},{12,16},{16,20},{20,24},{24,28},{1,5},{5,9},{9,... | collective-permute-start | bytes 12488 | tf_op jit(solution)/shard_map/ppermute | solution.py:13
  67.1 6.7 %collective-permute-start.11 = (f32[8,130,1]{1,0,2:T(8,128)S(1)}, f32[8,130,1]{1,0,2:T(8,128)S(1)}, u32[]{:S(2)}, u32[]{:S(2)}) collective-permute-start(f32[8,130,1]{1,0,2:T(8,128)S(1)} %copy.19), channel_id=1, source_target_pairs={{4,0},{8,4},{12,8},{16,12},{20,16},{24,20},{28,24},{5,1},{9,5},{13... | collective-permute-start | bytes 12488 | tf_op jit(solution)/shard_map/ppermute | solution.py:16
  76.8 7.7 %copy-start = (f32[8,128,256]{2,0,1:T(8,128)}, f32[8,128,256]{2,0,1:T(8,128)S(1)}, u32[]{:S(2)}) copy-start(f32[8,128,256]{2,0,1:T(8,128)S(1)} %fusion.27) | copy-start | bytes 3145732
  76.8 6.2 %collective-permute-start.13 = (f32[8,1,256]{2,0,1:T(8,128)S(1)}, f32[8,1,256]{2,0,1:T(8,128)S(1)}, u32[]{:S(2)}, u32[]{:S(2)}) collective-permute-start(f32[8,1,256]{2,0,1:T(8,128)S(1)} %get-tuple-element.19), channel_id=1, source_target_pairs={{32,0},{64,32},{96,64},{128,96},{160,128},{192,160},{224,192},{33,... | collective-permute-start | bytes 24584 | tf_op jit(solution)/shard_map/ppermute | solution.py:16
  78.2 6.3 %collective-permute-start.12 = (f32[8,1,256]{2,0,1:T(8,128)S(1)}, f32[8,1,256]{2,0,1:T(8,128)S(1)}, u32[]{:S(2)}, u32[]{:S(2)}) collective-permute-start(f32[8,1,256]{2,0,1:T(8,128)S(1)} %get-tuple-element.20), channel_id=1, source_target_pairs={{0,32},{32,64},{64,96},{96,128},{128,160},{160,192},{192,224},{1,3... | collective-permute-start | bytes 24584 | tf_op jit(solution)/shard_map/ppermute | solution.py:13
  85.5 8.5 %copy-start.2 = (f32[5]{0:T(128)S(1)}, f32[5]{0:T(128)}, u32[]{:S(2)}) copy-start(f32[5]{0:T(128)} %param.9) | copy-start | bytes 64
  87.3 9.3 %collective-permute-start.15 = (f32[8,130,1]{1,0,2:T(8,128)S(1)}, f32[8,130,1]{1,0,2:T(8,128)S(1)}, u32[]{:S(2)}, u32[]{:S(2)}) collective-permute-start(f32[8,130,1]{1,0,2:T(8,128)S(1)} %copy.23), channel_id=1, source_target_pairs={{4,0},{8,4},{12,8},{16,12},{20,16},{24,20},{28,24},{5,1},{9,5},{13... | collective-permute-start | bytes 12488 | tf_op jit(solution)/shard_map/ppermute | solution.py:16
  88.6 6.8 %collective-permute-start.14 = (f32[8,130,1]{1,0,2:T(8,128)S(1)}, f32[8,130,1]{1,0,2:T(8,128)S(1)}, u32[]{:S(2)}, u32[]{:S(2)}) collective-permute-start(f32[8,130,1]{1,0,2:T(8,128)S(1)} %copy.21), channel_id=1, source_target_pairs={{0,4},{4,8},{8,12},{12,16},{16,20},{20,24},{24,28},{1,5},{5,9},{9,... | collective-permute-start | bytes 12488 | tf_op jit(solution)/shard_map/ppermute | solution.py:13
  106.1 7.3 %collective-permute-start.17 = (f32[8,1,256]{2,0,1:T(8,128)S(1)}, f32[8,1,256]{2,0,1:T(8,128)S(1)}, u32[]{:S(2)}, u32[]{:S(2)}) collective-permute-start(f32[8,1,256]{2,0,1:T(8,128)S(1)} %get-tuple-element.17), channel_id=1, source_target_pairs={{32,0},{64,32},{96,64},{128,96},{160,128},{192,160},{224,192},{33,... | collective-permute-start | bytes 24584 | tf_op jit(solution)/shard_map/ppermute | solution.py:16
  107.4 7.4 %collective-permute-start.16 = (f32[8,1,256]{2,0,1:T(8,128)S(1)}, f32[8,1,256]{2,0,1:T(8,128)S(1)}, u32[]{:S(2)}, u32[]{:S(2)}) collective-permute-start(f32[8,1,256]{2,0,1:T(8,128)S(1)} %get-tuple-element.18), channel_id=1, source_target_pairs={{0,32},{32,64},{64,96},{96,128},{128,160},{160,192},{192,224},{1,3... | collective-permute-start | bytes 24584 | tf_op jit(solution)/shard_map/ppermute | solution.py:13
  115.4 6.7 %collective-permute-start.18 = (f32[8,130,1]{1,0,2:T(8,128)S(1)}, f32[8,130,1]{1,0,2:T(8,128)S(1)}, u32[]{:S(2)}, u32[]{:S(2)}) collective-permute-start(f32[8,130,1]{1,0,2:T(8,128)S(1)} %copy.25), channel_id=1, source_target_pairs={{0,4},{4,8},{8,12},{12,16},{16,20},{20,24},{24,28},{1,5},{5,9},{9,... | collective-permute-start | bytes 12488 | tf_op jit(solution)/shard_map/ppermute | solution.py:13
  120.6 6.7 %collective-permute-start.19 = (f32[8,130,1]{1,0,2:T(8,128)S(1)}, f32[8,130,1]{1,0,2:T(8,128)S(1)}, u32[]{:S(2)}, u32[]{:S(2)}) collective-permute-start(f32[8,130,1]{1,0,2:T(8,128)S(1)} %copy.27), channel_id=1, source_target_pairs={{4,0},{8,4},{12,8},{16,12},{20,16},{24,20},{28,24},{5,1},{9,5},{13... | collective-permute-start | bytes 12488 | tf_op jit(solution)/shard_map/ppermute | solution.py:16
Sparse Core Ops, SparseCore 0:
  131.9 71.4 all-gather.1
